TPU v7x, 512 devices: a whole 4x8x8 slice. The times are simulated.
512 devices in a mesh: gx: 32 (over x, y), gy: 16 (over z, core).
Axes of the slice: x: 4, y: 8, z: 8, core: 2. Of those that a mesh axis runs over, the one named last changes fastest.
Arguments:
- field: float32 [4, 8192, 8192], P(None, 'gx', 'gy'), may hold values from -6 to 6
- second_factor: float32 [8192, 32], P('gy'), may hold values from -0.0625 to 0.0625
- third_factor: float32 [4, 32], replicated, may hold values from -3 to 3
- first_factor: float32 [8192, 32], P(('gx', 'gy')), may hold values from -0.0625 to 0.0625
Outputs:
- new_factor: float32 [8192, 32], P(('gx', 'gy'))
- core: float32 [32, 32, 32], replicated
All inputs are finite; a program needn't handle non-finite values.
Results may differ from a plain program's by a relative error of at most 0.00027.
Values sent between devices are 32-bit elements; how exact they have to be, the bound alone decides.
A program may use at most 64 MiB of HBM per device.

v0:
```python
import jax
import jax.numpy as jnp
from jax import lax
from jax.sharding import PartitionSpec as P

HIGHEST_PRECISION = lax.Precision.HIGHEST


def on_device(field, second_factor, third_factor, first_factor):
    height = field.shape[1]
    factor_rank = second_factor.shape[1]
    share_rows = height // lax.axis_size("gy")
    total_rows = jnp.float32(height * lax.axis_size("gx"))
    reduced_two = jnp.einsum("kij,ja->kia", field, second_factor, precision=HIGHEST_PRECISION)
    joined_modes = jnp.einsum("kia,kb->iab", reduced_two, third_factor, precision=HIGHEST_PRECISION)
    basis_rows = lax.psum_scatter(
        joined_modes.reshape(share_rows * lax.axis_size("gy"), factor_rank * factor_rank),
        "gy",
        scatter_dimension=0,
        tiled=True,
    )
    local_probe = jnp.dot(basis_rows.T, first_factor, precision=HIGHEST_PRECISION)
    probe_summed = lax.psum(local_probe, ("gx", "gy"))
    mixed_rows = jnp.dot(basis_rows, probe_summed, precision=HIGHEST_PRECISION)
    local_gram = jnp.dot(mixed_rows.T, mixed_rows, precision=HIGHEST_PRECISION)
    gram_matrix = lax.psum(local_gram, ("gx", "gy"))
    lower_factor = jnp.linalg.cholesky(gram_matrix / total_rows)
    new_factor = jax.scipy.linalg.solve_triangular(lower_factor, mixed_rows.T, lower=True).T
    local_core = jnp.dot(new_factor.T, basis_rows, precision=HIGHEST_PRECISION)
    core_flat = lax.psum(local_core, ("gx", "gy")) / total_rows
    return (new_factor, core_flat.reshape(factor_rank, factor_rank, factor_rank))


def solution(mesh):
    return jax.shard_map(
        on_device,
        mesh=mesh,
        in_specs=(P(None, "gx", "gy"), P("gy", None), P(), P(("gx", "gy"), None)),
        out_specs=(P(("gx", "gy"), None), P()),
        check_vma=False,
    )
```

profile of v0, /device:TPU:1, one launch (start us, length us, event | category | flops | bytes accessed | tf_op | source)
XLA Modules:
  0.0 732.8 jit_solution(13375798610218987283)
XLA Ops:
  7.2 0.0 copy-start
  7.2 0.0 copy-start.3
  7.2 0.0 reduce-scatter.4.cloned.1.call-start
  7.2 1.5 copy-done
  8.8 2.9 fusion.2
  11.6 0.0 copy-done.3
  11.6 0.0 copy-start.2
  11.6 1.0 fusion
  12.7 1.3 copy.12
  14.0 0.0 reduce-scatter.4.cloned.1.call-update
  14.0 0.0 all-reduce.3.cloned.1.call-start
  14.1 64.6 %reduce-scatter.4.cloned.1.call-done = f32[16,1024]{1,0:T(8,128)} async-done(((f32[256,1024]{1,0:T(8,128)}), f32[16,1024]{1,0:T(8,128)}) %reduce-scatter.4.cloned.1.call-update) | async-done | bytes 65552
  78.7 0.0 copy-done.2
  78.7 2.6 fusion.9
  81.3 0.0 all-reduce.3.cloned.1.call-update
  81.3 0.0 all-reduce.5.cloned.1.call-start
  81.4 276.0 %all-reduce.3.cloned.1.call-done = f32[1024,32]{1,0:T(8,128)} async-done(((f32[1024,32]{1,0:T(8,128)}), f32[1024,32]{1,0:T(8,128)}) %all-reduce.3.cloned.1.call-update) | async-done | bytes 131088 | tf_op jit(solution)/shard_map/psum | solution.py:23
  357.4 1.4 fusion.10
  358.8 0.2 fusion.11
  359.1 97.2 %psum.22 = f32[32,32]{0,1:T(8,128)S(1)} all-reduce(f32[32,32]{0,1:T(8,128)S(1)} %fusion.11), channel_id=1, replica_groups=mesh['gx'=32,'gy'=16] {'gx','gy'}, use_global_device_ids=true, to_apply=%region_2.0 | all-reduce | flops 1024 | bytes 8192 | tf_op jit(solution)/shard_map/psum | solution.py:26
  456.3 0.1 copy.9
  456.3 2.9 cholesky.16
  459.3 0.6 compare_reduce_fusion
  459.9 0.7 fusion.4
  460.6 2.4 custom-call.7
  463.0 0.2 fusion.5
  463.2 0.0 copy-start.1
  463.2 1.8 fusion.12
  465.0 0.0 all-reduce.5.cloned.1.call-update
  465.0 259.3 %all-reduce.5.cloned.1.call-done = f32[32,1024]{1,0:T(8,128)} async-done(((f32[32,1024]{1,0:T(8,128)}), f32[32,1024]{1,0:T(8,128)}) %all-reduce.5.cloned.1.call-update) | async-done | bytes 131088 | tf_op jit(solution)/shard_map/psum | solution.py:30
  724.4 0.9 broadcast_multiply_fusion
  725.3 1.0 reshape.21
  726.2 0.0 copy-done.1
  (3 shorter events, 0.0 us)
Async XLA Ops:
  7.2 1.6 copy-start
  7.2 4.4 copy-start.3
  7.2 71.5 %reduce-scatter.4.cloned.1.call-start = ((), (), s32[]{:S(2)}) async-start(), calls=%async_computation.3 | async-start | bytes 1114112
  11.6 67.0 %copy-start.2 = (f32[16,32]{1,0:T(8,128)S(1)}, f32[16,32]{1,0:T(8,128)}, u32[]{:S(2)}) copy-start(f32[16,32]{1,0:T(8,128)} %param.7) | copy-start | bytes 6148
  14.0 343.4 %all-reduce.3.cloned.1.call-start = ((), (), s32[]{:S(2)}) async-start(), calls=%async_computation.1 | async-start | bytes 1048576 | tf_op jit(solution)/shard_map/psum | solution.py:23
  81.3 643.0 %all-reduce.5.cloned.1.call-start = ((), (), s32[]{:S(2)}) async-start(), calls=%async_computation.2 | async-start | bytes 262144 | tf_op jit(solution)/shard_map/psum | solution.py:30
  463.2 263.1 %copy-start.1 = (f32[32,16]{0,1:T(8,128)}, f32[32,16]{0,1:T(8,128)S(1)}, u32[]{:S(2)}) copy-start(f32[32,16]{0,1:T(8,128)S(1)} %fusion.5) | copy-start | bytes 6148
Sparse Core Ops, SparseCore 0:
  14.2 64.4 reduce-scatter.3
  84.2 273.1 all-reduce.2
  465.2 259.1 all-reduce.4
where the time goes:
time: 733 us
  waiting for transfers between devices  600 us (82%)
  blocking collectives  97.2 us (13%)
  between operations  13.8 us (2%)
  matrix products  10.1 us (1%)
  other arithmetic  7.61 us (1%)
    psum x1, waiting for transfers between devices, on_device(): probe_summed = lax.psum(local_probe, ('gx', 'gy'))  276 us
    psum x1, waiting for transfers between devices, on_device(): core_flat = lax.psum(local_core, ('gx', 'gy')) / total_rows  259 us
    psum x1, blocking collectives, on_device(): gram_matrix = lax.psum(local_gram, ('gx', 'gy'))  97.2 us
    unnamed x4, waiting for transfers between devices  64.6 us
  transfers between devices with their start and end apart: 3, of which 3 were waited for; matrix products, arithmetic and copies ran while one was open for 0% of the time, Pallas kernels for 0%

commit v1 on v0

v1 whole, which is shorter than its diff:
```python
import jax
import jax.numpy as jnp
from jax import lax
from jax.sharding import PartitionSpec as P

HIGHEST = lax.Precision.HIGHEST


def on_device(field, second_factor, third_factor, first_factor):
    planes, height, _ = field.shape
    rank = second_factor.shape[1]
    total_rows = jnp.float32(height * lax.axis_size("gx"))
    inner = jnp.einsum("kij,ja->ika", field, second_factor, precision=HIGHEST)
    rows = lax.psum_scatter(inner.reshape(height, planes * rank), "gy", scatter_dimension=0, tiled=True)
    both = jnp.concatenate([rows, first_factor], axis=1)
    summed = lax.psum(jnp.dot(rows.T, both, precision=HIGHEST), ("gx", "gy"))
    square = summed[:, : planes * rank]
    probe = summed[:, planes * rank :].reshape(planes, rank, rank)
    plane_gram = jnp.dot(third_factor, third_factor.T, precision=HIGHEST)
    weights = jnp.einsum("kl,lac->kac", plane_gram, probe, precision=HIGHEST).reshape(planes * rank, rank)
    projected = jnp.dot(weights.T, square, precision=HIGHEST)
    gram = jnp.dot(projected, weights, precision=HIGHEST) / total_rows
    lower = jnp.linalg.cholesky(gram)
    inverse = jax.scipy.linalg.solve_triangular(lower, jnp.eye(rank, dtype=jnp.float32), lower=True)
    new_factor = jnp.dot(rows, jnp.dot(weights, inverse.T, precision=HIGHEST), precision=HIGHEST)
    slim = jnp.dot(inverse, projected, precision=HIGHEST).reshape(rank, planes, rank)
    core = jnp.einsum("cka,kb->cab", slim, third_factor, precision=HIGHEST) / total_rows
    return (new_factor, core)


def solution(mesh):
    return jax.shard_map(
        on_device,
        mesh=mesh,
        in_specs=(P(None, "gx", "gy"), P("gy", None), P(), P(("gx", "gy"), None)),
        out_specs=(P(("gx", "gy"), None), P()),
        check_vma=False,
    )
```

time: 733 us -> 365 us (0.50)
  waiting for transfers between devices: 600 us -> 331 us
  blocking collectives: 97.2 us -> 0 us
    psum x2 -> x1, waiting for transfers between devices: 535 us -> 268 us  [on_device(): summed = lax.psum(jnp.dot(rows.T, both, precision=HIGHEST), ('gx', 'gy'))]
    psum x1 -> x0, blocking collectives: 97.2 us -> none  [on_device(): gram_matrix = lax.psum(local_gram, ('gx', 'gy'))]
    unnamed x4 -> x3, waiting for transfers between devices: 64.6 us -> 63.1 us
  transfers between devices with their start and end apart: 3 -> 2, of which waited for: 3 -> 2; matrix products, arithmetic and copies ran while one was open for 0% -> 0% of each run, Pallas kernels for 0% -> 0%
where the time goes in v1:
time: 365 us
  waiting for transfers between devices  331 us (91%)
  between operations  14.1 us (4%)
  matrix products  9.94 us (3%)
  other arithmetic  6.69 us (2%)
    psum x1, waiting for transfers between devices, on_device(): summed = lax.psum(jnp.dot(rows.T, both, precision=HIGHEST), ('gx', 'gy'))  268 us
    unnamed x3, waiting for transfers between devices  63.1 us
  transfers between devices with their start and end apart: 2, of which 2 were waited for; matrix products, arithmetic and copies ran while one was open for 0% of the time, Pallas kernels for 0%

profile of v1, /device:TPU:1, one launch (start us, length us, event | category | flops | bytes accessed | tf_op | source)
XLA Modules:
  0.0 365.0 jit_solution(15570193730664428700)
XLA Ops:
  7.2 0.0 copy-start
  7.2 0.0 copy-start.2
  7.2 0.0 copy-start.1
  7.2 0.0 reduce-scatter.4.cloned.1.call-start
  7.2 1.5 copy-done
  8.8 2.8 fusion.2
  11.6 0.8 copy.19
  12.4 0.0 reduce-scatter.4.cloned.1.call-update
  12.4 0.0 all-reduce.2.cloned.1.call-start
  12.4 63.1 %reduce-scatter.4.cloned.1.call-done = f32[16,128]{1,0:T(8,128)} async-done(((f32[256,128]{1,0:T(8,128)}), f32[16,128]{1,0:T(8,128)}) %reduce-scatter.4.cloned.1.call-update) | async-done | bytes 8208
  75.6 0.0 copy-done.2
  75.6 1.7 fusion.5
  77.3 0.0 all-reduce.2.cloned.1.call-update
  77.3 0.0 copy-done.1
  77.3 0.1 convolution_bitcast_fusion
  77.5 267.6 %all-reduce.2.cloned.1.call-done = f32[128,160]{0,1:T(8,128)} async-done(((f32[128,160]{0,1:T(8,128)}), f32[128,160]{0,1:T(8,128)}) %all-reduce.2.cloned.1.call-update) | async-done | bytes 81936 | tf_op jit(solution)/shard_map/psum | solution.py:16
  345.1 0.7 slice.20
  345.8 0.1 reshape.27
  345.9 0.3 fusion.14
  346.1 0.1 reshape.28
  346.2 1.0 fusion
  347.3 0.2 fusion.15
  347.5 0.1 copy.16
  347.5 2.9 cholesky.17
  350.5 0.6 compare_reduce_fusion
  351.1 0.7 fusion.4
  351.8 2.4 custom-call.7
  354.2 0.2 fusion.9
  354.5 0.1 fusion.18
  354.6 0.2 fusion.16
  354.8 0.1 reshape.29
  354.9 1.8 convolution_multiply_fusion
  356.7 1.4 fusion.17
  (2 shorter events, 0.0 us)
Async XLA Ops:
  7.2 1.6 copy-start
  7.2 68.4 %copy-start.2 = (f32[16,32]{1,0:T(8,128)S(1)}, f32[16,32]{1,0:T(8,128)}, u32[]{:S(2)}) copy-start(f32[16,32]{1,0:T(8,128)} %param.7) | copy-start | bytes 6148
  7.2 70.1 %copy-start.1 = (f32[4,32]{1,0:T(4,128)S(1)}, f32[4,32]{1,0:T(4,128)}, u32[]{:S(2)}) copy-start(f32[4,32]{1,0:T(4,128)} %param.6) | copy-start | bytes 1540
  7.2 68.4 %reduce-scatter.4.cloned.1.call-start = ((), (), s32[]{:S(2)}) async-start(), calls=%async_computation.2 | async-start | bytes 139264
  12.4 332.7 %all-reduce.2.cloned.1.call-start = ((), (), s32[]{:S(2)}) async-start(), calls=%async_computation.1 | async-start | bytes 163840 | tf_op jit(solution)/shard_map/psum | solution.py:16
Sparse Core Ops, SparseCore 0:
  12.5 62.9 reduce-scatter.3
  81.1 263.9 all-reduce.1

commit v2 on v1

v2 whole, which is shorter than its diff:
```python
import functools

import jax
import jax.numpy as jnp
from jax import lax
from jax.experimental import pallas as pl
from jax.experimental.pallas import tpu as pltpu
from jax.sharding import PartitionSpec as P

HIGHEST = lax.Precision.HIGHEST
MESH = pl.DeviceIdType.MESH
NN = (((1,), (0,)), ((), ()))
NT = (((1,), (1,)), ((), ()))
TN = (((0,), (0,)), ((), ()))
TT = (((0,), (1,)), ((), ()))


def exact(a, b, dims):
    return lax.dot_general(a, b, dims, precision=HIGHEST, preferred_element_type=jnp.float32)


def split(a):
    high = a.astype(jnp.bfloat16)
    return high, (a - high.astype(jnp.float32)).astype(jnp.bfloat16)


def exchange_kernel(
    nx, ny, nz,
    field_ref, second_ref, first_ref, total_ref, rows_ref,
    planes, second, weights, first, partial, arrived, local, scattered, stage, final,
    load_sem, small_sem, send1, recv1, send2, recv2, send3, recv3, send4, recv4,
):
    gx, gy = lax.axis_index("gx"), lax.axis_index("gy")
    x, y = gx // ny, gx % ny
    z, core = gy // 2, gy % 2
    share = rows_ref.shape[0]
    width = rows_ref.shape[1]
    rank = second_ref.shape[0]
    parts = 2 * nx
    piece = width // parts
    half = piece // 2

    steps = sorted(range(nz), key=lambda o: -min(o, nz - o))
    owners = [lax.rem(z + o, nz) for o in steps]
    small = pltpu.make_async_copy(second_ref, second, small_sem.at[0])
    small.start()
    loads = []
    for s in range(nz):
        span = pl.ds(pl.multiple_of(owners[s] * (2 * share), 2 * share), 2 * share)
        loads.append(pltpu.make_async_copy(field_ref.at[:, span, :], planes.at[s], load_sem.at[s]))
        loads[-1].start()
    small_first = pltpu.make_async_copy(first_ref, first, small_sem.at[1])
    small_first.start()

    barrier = pltpu.get_barrier_semaphore()
    column = [(gx, lax.rem(gy + o, 2 * nz)) for o in range(1, 2 * nz)]
    plates = [(lax.rem(x + o, nx) * ny + y, z * 2 + c) for o in range(1, nx) for c in range(2)]
    lines = [(x * ny + lax.rem(y + o, ny), gy) for o in range(1, ny)]
    for peer in column + plates + lines:
        pl.semaphore_signal(barrier, inc=1, device_id=peer, device_id_type=MESH)

    small.wait()
    high, low = split(second[...])
    copies = width // rank
    weights[...] = jnp.concatenate([high] * copies + [low] * copies, axis=0)
    lane = lax.broadcasted_iota(jnp.int32, (2 * share, width), 1) // rank

    sends = []
    for s in range(nz):
        loads[s].wait()
        block = planes[s].reshape(copies * 2 * share, planes.shape[-1])
        high, low = split(block)
        near = lax.dot_general(high, weights[...], NT, preferred_element_type=jnp.float32)
        fine = lax.dot_general(low, weights[:width, :], NT, preferred_element_type=jnp.float32)
        acc = (near[:, :width] + (near[:, width:] + fine)).reshape(copies, 2 * share, width)
        out = acc[0]
        for k in range(1, copies):
            out = jnp.where(lane == k, acc[k], out)
        partial[s] = out
        if s == 0:
            pl.semaphore_wait(barrier, len(column + plates + lines))
        offset = steps[s]
        for flip in range(2):
            if offset == 0 and flip == 0:
                continue
            target = lax.rem(core + flip, 2)
            slot = offset * 2 + flip
            copy = pltpu.make_async_remote_copy(
                src_ref=partial.at[s, pl.ds(pl.multiple_of(target * share, share), share)],
                dst_ref=arrived.at[slot],
                send_sem=send1.at[slot],
                recv_sem=recv1.at[slot],
                device_id=(gx, owners[s] * 2 + target),
                device_id_type=MESH,
            )
            copy.start()
            sends.append(copy)

    own = partial[nz - 1, pl.ds(pl.multiple_of(core * share, share), share), :]
    for copy in reversed(sends):
        copy.wait_recv()
    rows = own
    for slot in range(1, 2 * nz):
        rows = rows + arrived[slot]
    rows_ref[...] = rows

    small_first.wait()
    square = exact(rows, rows, TN)
    probe = exact(first[...], rows, TN)
    second_rows, third_rows, last_rows = (square[k * rank : (k + 1) * rank] for k in range(1, 4))
    corner = lax.broadcasted_iota(jnp.int32, (rank, width), 1) < rank
    packed = jnp.where(corner, pltpu.roll(last_rows, rank, 1), second_rows)
    for at, rows_at in enumerate((square[:rank], packed, third_rows, probe)):
        for j in range(rank // piece):
            local[at * (rank // piece) + j] = rows_at[j * piece : (j + 1) * piece]

    mine = x * 2 + core
    sends2 = []
    for o in sorted(range(nx), key=lambda o: -min(o, nx - o)):
        for flip in range(2):
            if o == 0 and flip == 0:
                continue
            to_x, to_core = lax.rem(x + o, nx), lax.rem(core + flip, 2)
            slot = o * 2 + flip
            copy = pltpu.make_async_remote_copy(
                src_ref=local.at[to_x * 2 + to_core],
                dst_ref=scattered.at[slot],
                send_sem=send2.at[slot],
                recv_sem=recv2.at[slot],
                device_id=(to_x * ny + y, z * 2 + to_core),
                device_id_type=MESH,
            )
            copy.start()
            sends2.append(copy)
    for copy in reversed(sends2):
        copy.wait_recv()
    summed = local[mine]
    for slot in range(1, parts):
        summed = summed + scattered[slot]

    sends3 = []
    halves = [summed[:half], summed[half:]]
    for turn in range(2):
        arrivals = []
        for h in range(2):
            along_y = (turn + h) % 2 == 0
            count, me = (ny, y) if along_y else (nz, z)
            stage[turn, h, me] = halves[h]
            incoming = []
            for o in sorted(range(1, count), key=lambda o: -min(o, count - o)):
                to = lax.rem(me + o, count)
                peer = (x * ny + to, gy) if along_y else (gx, to * 2 + core)
                copy = pltpu.make_async_remote_copy(
                    src_ref=stage.at[turn, h, me],
                    dst_ref=stage.at[turn, h, me],
                    send_sem=send3.at[turn, h, o],
                    recv_sem=recv3.at[turn, h, o],
                    device_id=peer,
                    device_id_type=MESH,
                )
                copy.start()
                incoming.append(copy)
            sends3 += incoming
            arrivals.append((count, incoming))
        for h in range(2):
            count, incoming = arrivals[h]
            for copy in reversed(incoming):
                copy.wait_recv()
            value = stage[turn, h, 0]
            for j in range(1, count):
                value = value + stage[turn, h, j]
            halves[h] = value

    final[mine, :half] = halves[0]
    final[mine, half:] = halves[1]
    sends4 = []
    for o in sorted(range(nx), key=lambda o: -min(o, nx - o)):
        for flip in range(2):
            if o == 0 and flip == 0:
                continue
            slot = o * 2 + flip
            copy = pltpu.make_async_remote_copy(
                src_ref=final.at[mine],
                dst_ref=final.at[mine],
                send_sem=send4.at[slot],
                recv_sem=recv4.at[slot],
                device_id=(lax.rem(x + o, nx) * ny + y, z * 2 + lax.rem(core + flip, 2)),
                device_id_type=MESH,
            )
            copy.start()
            sends4.append(copy)
    for copy in reversed(sends4):
        copy.wait_recv()
    total_ref[...] = final[...].reshape(width, width)
    for copy in sends + sends2 + sends3 + sends4:
        copy.wait_send()


def finish_kernel(count, total_ref, rows_ref, third_ref, factor_ref, core_ref):
    planes, rank = third_ref.shape
    width = planes * rank
    third = third_ref[...]
    repeated = jnp.concatenate([jnp.broadcast_to(third[k : k + 1], (rank, rank)) for k in range(planes)], axis=0)
    row = lax.broadcasted_iota(jnp.int32, (width, width), 0)
    column = lax.broadcasted_iota(jnp.int32, (width, width), 1)
    kron = jnp.where(row % rank == column % rank, exact(repeated, repeated, NT), 0.0)

    total = total_ref[...]
    probe = total[3 * rank :]
    middle = total[rank : 2 * rank]
    zero = jnp.zeros((rank, width), jnp.float32)
    lane = lax.broadcasted_iota(jnp.int32, (rank, width), 1) // rank
    last = jnp.where(lane == 3, pltpu.roll(middle, 3 * rank, 1), zero)
    blocks = [
        total[:rank],
        jnp.where(lane >= 1, middle, zero),
        jnp.where(lane >= 2, total[2 * rank : 3 * rank], zero),
        last,
    ]
    upper = jnp.concatenate(blocks, axis=0)
    strict = jnp.concatenate([jnp.where(lane > k, blocks[k], zero) for k in range(planes)], axis=0)
    weights = exact(probe, kron, NN)
    projected = exact(weights, upper, NN) + exact(weights, strict, NT)
    gram = exact(projected, weights, NT) / count
    mixed = exact(rows_ref[...], weights, NT)

    at = lax.broadcasted_iota(jnp.int32, (rank, rank), 0)
    across = lax.broadcasted_iota(jnp.int32, (rank, rank), 1)
    state = jnp.concatenate([gram, jnp.where(at == across, 1.0, 0.0)], axis=1)
    below = lax.broadcasted_iota(jnp.int32, (rank, 2 * rank), 0)
    pivots = jnp.ones((rank, 2 * rank), jnp.float32)
    for k in range(rank):
        line = jnp.broadcast_to(state[k : k + 1], (rank, 2 * rank))
        pivot = jnp.broadcast_to(state[k : k + 1, k : k + 1], (rank, 2 * rank))
        ratio = jnp.broadcast_to(state[:, k : k + 1], (rank, 2 * rank)) / pivot
        pivots = jnp.where(below == k, pivot, pivots)
        state = jnp.where(below > k, state - ratio * line, state)
    inverse = (state / jnp.sqrt(pivots))[:, rank:]

    factor_ref[...] = exact(mixed, inverse, NT)
    slim = exact(projected, inverse / count, TT)
    for c in range(rank):
        terms = slim[:, c : c + 1] * repeated
        core_ref[c] = (terms[:rank] + terms[rank : 2 * rank]) + (terms[2 * rank : 3 * rank] + terms[3 * rank :])


def on_device(nx, ny, nz, total_rows, field, second_factor, third_factor, first_factor):
    planes, height, depth = field.shape
    rank = second_factor.shape[1]
    share = first_factor.shape[0]
    width = planes * rank
    parts = 2 * nx
    piece = width // parts
    longest = max(ny, nz)
    anywhere = pl.BlockSpec(memory_space=pl.ANY)
    inside = pl.BlockSpec(memory_space=pltpu.VMEM)
    dma = pltpu.SemaphoreType.DMA
    total, rows = pl.pallas_call(
        functools.partial(exchange_kernel, nx, ny, nz),
        out_shape=(
            jax.ShapeDtypeStruct((width, width), jnp.float32),
            jax.ShapeDtypeStruct((share, width), jnp.float32),
        ),
        in_specs=[anywhere] * 3,
        out_specs=[inside] * 2,
        scratch_shapes=[
            pltpu.VMEM((nz, planes, 2 * share, depth), jnp.float32),
            pltpu.VMEM((rank, depth), jnp.float32),
            pltpu.VMEM((2 * width, depth), jnp.bfloat16),
            pltpu.VMEM((share, rank), jnp.float32),
            pltpu.VMEM((nz, 2 * share, width), jnp.float32),
            pltpu.VMEM((2 * nz, share, width), jnp.float32),
            pltpu.VMEM((parts, piece, width), jnp.float32),
            pltpu.VMEM((parts, piece, width), jnp.float32),
            pltpu.VMEM((2, 2, longest, piece // 2, width), jnp.float32),
            pltpu.VMEM((parts, piece, width), jnp.float32),
            dma((nz,)),
            dma((2,)),
            dma((2 * nz,)),
            dma((2 * nz,)),
            dma((parts,)),
            dma((parts,)),
            dma((2, 2, longest)),
            dma((2, 2, longest)),
            dma((parts,)),
            dma((parts,)),
        ],
        compiler_params=pltpu.CompilerParams(collective_id=0, has_side_effects=True),
        name="exchange",
    )(field, second_factor.T, first_factor)
    return pl.pallas_call(
        functools.partial(finish_kernel, float(total_rows)),
        out_shape=(
            jax.ShapeDtypeStruct((share, rank), jnp.float32),
            jax.ShapeDtypeStruct((rank, rank, rank), jnp.float32),
        ),
        in_specs=[inside] * 3,
        out_specs=[inside] * 2,
        name="finish",
    )(total, rows, third_factor)


def build(mesh, nx, ny, nz, total_rows):
    return jax.shard_map(
        functools.partial(on_device, nx, ny, nz, total_rows),
        mesh=mesh,
        in_specs=(P(None, "gx", "gy"), P("gy", None), P(), P(("gx", "gy"), None)),
        out_specs=(P(("gx", "gy"), None), P()),
        check_vma=False,
    )


def solution(mesh):
    ny = 8
    return build(mesh, mesh.shape["gx"] // ny, ny, mesh.shape["gy"] // 2, 8192)
```

time: 365 us -> 48.3 us (0.13)
  waiting for transfers between devices: 331 us -> 0 us
  Pallas kernels: 0 us -> 47.5 us
  between operations: 14.1 us -> 0.64 us
  matrix products: 9.94 us -> 0 us
  other arithmetic: 6.69 us -> 0 us
    psum x1 -> x0, waiting for transfers between devices: 268 us -> none  [on_device(): summed = lax.psum(jnp.dot(rows.T, both, precision=HIGHEST), ('gx', 'gy'))]
    unnamed x3 -> x0, waiting for transfers between devices: 63.1 us -> none
    pallas_call x0 -> x2, Pallas kernels: none -> 47.5 us  [the longest x1 39.8 us: on_device(): pl.pallas_call(functools.partial(exchange_kernel, nx, ny, nz), out_shape=...]
    dot_general x10 -> x0, matrix products: 9.72 us -> none  [the longest x1 2.84 us: on_device(): inner = jnp.einsum('kij,ja->ika', field, second_factor, precision=HIGHEST)]
    another operation x5 -> x0, other arithmetic: 6.69 us -> none  [the longest x3 3.6 us: on_device(): lower = jnp.linalg.cholesky(gram)]
  transfers between devices with their start and end apart: 2 -> 0, of which waited for: 2 -> 0; matrix products, arithmetic and copies ran while one was open for 0% -> 0% of each run, Pallas kernels for 0% -> 0%
where the time goes in v2:
time: 48.3 us; the launch traced here: 48.1 us
  Pallas kernels  47.5 us (98%)
  between operations  0.64 us (1%)
    pallas_call x1, Pallas kernels, on_device(): pl.pallas_call(functools.partial(exchange_kernel, nx, ny, nz), out_shape=...  39.8 us
    pallas_call x1, Pallas kernels, on_device(): pl.pallas_call(functools.partial(finish_kernel, float(total_rows)), out_s...  7.74 us

profile of v2, /device:TPU:1, one launch (start us, length us, event | category | flops | bytes accessed | tf_op | source)
XLA Modules:
  0.0 48.1 jit_solution(8576232554846709906)
XLA Ops:
  0.6 39.8 %exchange.1 = (f32[128,128]{1,0:T(8,128)}, f32[16,128]{1,0:T(8,128)}) custom-call(f32[4,256,512]{2,1,0:T(8,128)} %field_ref.1, f32[32,512]{1,0:T(8,128)} %bitcast.1, f32[16,32]{1,0:T(8,128)} %first_ref.1), custom_call_target="tpu_custom_call" | custom-call | tf_op jit(solution)/shard_map/exchange/pallas_call | solution.py:258
  40.4 7.7 %finish.1 = (f32[16,32]{1,0:T(8,128)}, f32[32,32,32]{2,1,0:T(8,128)}) custom-call(f32[128,128]{1,0:T(8,128)} %get-tuple-element.4.total_ref, f32[16,128]{1,0:T(8,128)} %get-tuple-element.5.rows_ref, f32[4,32]{1,0:T(4,128)} %third_ref.1), custom_call_target="tpu_custom_call" | custom-call | tf_op jit(solution)/shard_map/finish/pallas_call | solution.py:291

commit v3 on v2

--- a/solution.py
+++ b/solution.py
@@ -27,80 +27,103 @@
 def exchange_kernel(
     nx, ny, nz,
     field_ref, second_ref, first_ref, total_ref, rows_ref,
-    planes, second, weights, first, partial, arrived, local, scattered, stage, final,
-    load_sem, small_sem, send1, recv1, send2, recv2, send3, recv3, send4, recv4,
+    planes, second, weights, first, partial, paired, outgoing, arrived, local, scattered, stage, final,
+    load_sem, small_sem, send0, recv0, send1, recv1, send2, recv2, send3, recv3, send4, recv4,
 ):
     gx, gy = lax.axis_index("gx"), lax.axis_index("gy")
     x, y = gx // ny, gx % ny
     z, core = gy // 2, gy % 2
+    other = 1 - core
     share = rows_ref.shape[0]
     width = rows_ref.shape[1]
     rank = second_ref.shape[0]
+    copies = width // rank
     parts = 2 * nx
     piece = width // parts
     half = piece // 2
 
     steps = sorted(range(nz), key=lambda o: -min(o, nz - o))
+    group = nz // 2
     owners = [lax.rem(z + o, nz) for o in steps]
     small = pltpu.make_async_copy(second_ref, second, small_sem.at[0])
     small.start()
     loads = []
-    for s in range(nz):
-        span = pl.ds(pl.multiple_of(owners[s] * (2 * share), 2 * share), 2 * share)
-        loads.append(pltpu.make_async_copy(field_ref.at[:, span, :], planes.at[s], load_sem.at[s]))
-        loads[-1].start()
+    for turn in range(4):
+        whose = other if turn < 2 else core
+        for j in range(group):
+            load = pltpu.make_async_copy(
+                field_ref.at[:, owners[turn % 2 * group + j], whose], planes.at[turn, j], load_sem.at[turn, j]
+            )
+            load.start()
+            loads.append(load)
     small_first = pltpu.make_async_copy(first_ref, first, small_sem.at[1])
     small_first.start()
 
     barrier = pltpu.get_barrier_semaphore()
-    column = [(gx, lax.rem(gy + o, 2 * nz)) for o in range(1, 2 * nz)]
+    sibling = (gx, z * 2 + other)
+    column = [(gx, lax.rem(z + o, nz) * 2 + core) for o in range(1, nz)]
     plates = [(lax.rem(x + o, nx) * ny + y, z * 2 + c) for o in range(1, nx) for c in range(2)]
     lines = [(x * ny + lax.rem(y + o, ny), gy) for o in range(1, ny)]
-    for peer in column + plates + lines:
+    peers = [sibling] + column + plates + lines
+    for peer in peers:
         pl.semaphore_signal(barrier, inc=1, device_id=peer, device_id_type=MESH)
 
     small.wait()
     high, low = split(second[...])
-    copies = width // rank
     weights[...] = jnp.concatenate([high] * copies + [low] * copies, axis=0)
-    lane = lax.broadcasted_iota(jnp.int32, (2 * share, width), 1) // rank
+    lane = lax.broadcasted_iota(jnp.int32, (group, share, width), 2) // rank
 
     sends = []
-    for s in range(nz):
-        loads[s].wait()
-        block = planes[s].reshape(copies * 2 * share, planes.shape[-1])
-        high, low = split(block)
-        near = lax.dot_general(high, weights[...], NT, preferred_element_type=jnp.float32)
-        fine = lax.dot_general(low, weights[:width, :], NT, preferred_element_type=jnp.float32)
-        acc = (near[:, :width] + (near[:, width:] + fine)).reshape(copies, 2 * share, width)
-        out = acc[0]
+    pairs = []
+    for turn in range(4):
+        for load in loads[turn * group : (turn + 1) * group]:
+            load.wait()
+        count = group * copies * share
+        block = planes[turn].reshape(count, planes.shape[-1])
+        both = jnp.concatenate(split(block), axis=0)
+        product = lax.dot_general(both, weights[...], NT, preferred_element_type=jnp.float32)
+        acc = product[:count, :width] + (product[:count, width:] + product[count:, :width])
+        acc = acc.reshape(group, copies, share, width)
+        out = acc[:, 0]
         for k in range(1, copies):
-            out = jnp.where(lane == k, acc[k], out)
-        partial[s] = out
-        if s == 0:
-            pl.semaphore_wait(barrier, len(column + plates + lines))
-        offset = steps[s]
-        for flip in range(2):
-            if offset == 0 and flip == 0:
-                continue
-            target = lax.rem(core + flip, 2)
-            slot = offset * 2 + flip
+            out = jnp.where(lane == k, acc[:, k], out)
+        if turn < 2:
+            partial[turn] = out
+            if turn == 0:
+                pl.semaphore_wait(barrier, len(peers))
             copy = pltpu.make_async_remote_copy(
-                src_ref=partial.at[s, pl.ds(pl.multiple_of(target * share, share), share)],
-                dst_ref=arrived.at[slot],
-                send_sem=send1.at[slot],
-                recv_sem=recv1.at[slot],
-                device_id=(gx, owners[s] * 2 + target),
+                src_ref=partial.at[turn],
+                dst_ref=paired.at[turn],
+                send_sem=send0.at[turn],
+                recv_sem=recv0.at[turn],
+                device_id=sibling,
                 device_id_type=MESH,
             )
             copy.start()
-            sends.append(copy)
-
-    own = partial[nz - 1, pl.ds(pl.multiple_of(core * share, share), share), :]
+            pairs.append(copy)
+        else:
+            side = turn - 2
+            pairs[side].wait_recv()
+            outgoing[side] = out + paired[side]
+            for j in range(group):
+                offset = steps[side * group + j]
+                if offset == 0:
+                    continue
+                copy = pltpu.make_async_remote_copy(
+                    src_ref=outgoing.at[side, j],
+                    dst_ref=arrived.at[offset],
+                    send_sem=send1.at[offset],
+                    recv_sem=recv1.at[offset],
+                    device_id=(gx, owners[side * group + j] * 2 + core),
+                    device_id_type=MESH,
+                )
+                copy.start()
+                sends.append(copy)
+
     for copy in reversed(sends):
         copy.wait_recv()
-    rows = own
-    for slot in range(1, 2 * nz):
+    rows = outgoing[1, group - 1]
+    for slot in range(1, nz):
         rows = rows + arrived[slot]
     rows_ref[...] = rows
 
@@ -192,7 +215,7 @@
     for copy in reversed(sends4):
         copy.wait_recv()
     total_ref[...] = final[...].reshape(width, width)
-    for copy in sends + sends2 + sends3 + sends4:
+    for copy in pairs + sends + sends2 + sends3 + sends4:
         copy.wait_send()
 
 
@@ -226,16 +249,33 @@
 
     at = lax.broadcasted_iota(jnp.int32, (rank, rank), 0)
     across = lax.broadcasted_iota(jnp.int32, (rank, rank), 1)
-    state = jnp.concatenate([gram, jnp.where(at == across, 1.0, 0.0)], axis=1)
-    below = lax.broadcasted_iota(jnp.int32, (rank, 2 * rank), 0)
-    pivots = jnp.ones((rank, 2 * rank), jnp.float32)
-    for k in range(rank):
-        line = jnp.broadcast_to(state[k : k + 1], (rank, 2 * rank))
-        pivot = jnp.broadcast_to(state[k : k + 1, k : k + 1], (rank, 2 * rank))
-        ratio = jnp.broadcast_to(state[:, k : k + 1], (rank, 2 * rank)) / pivot
-        pivots = jnp.where(below == k, pivot, pivots)
-        state = jnp.where(below > k, state - ratio * line, state)
-    inverse = (state / jnp.sqrt(pivots))[:, rank:]
+    joined = jnp.concatenate([gram, jnp.where(at == across, 1.0, 0.0)], axis=1)
+    size = 8
+    groups = rank // size
+    shape = (size, 2 * rank)
+    state = [joined[g * size : (g + 1) * size] for g in range(groups)]
+    below = lax.broadcasted_iota(jnp.int32, shape, 0)
+    inverse = []
+    for b in range(groups):
+        columns = [
+            [jnp.broadcast_to(state[g][:, b * size + j : b * size + j + 1], shape) for g in range(b, groups)]
+            for j in range(size)
+        ]
+        pivots = jnp.ones(shape, jnp.float32)
+        for j in range(size):
+            pivot = jnp.broadcast_to(columns[j][0][j : j + 1], shape)
+            pivots = jnp.where(below == j, pivot, pivots)
+            scale = 1.0 / pivot
+            ratio = [part * scale for part in columns[j]]
+            ratio[0] = jnp.where(below > j, ratio[0], 0.0)
+            for later in range(j + 1, size):
+                top = jnp.broadcast_to(columns[later][0][j : j + 1], shape)
+                columns[later] = [part - r * top for part, r in zip(columns[later], ratio)]
+            line = jnp.broadcast_to(state[b][j : j + 1], shape)
+            for g in range(b, groups):
+                state[g] = state[g] - ratio[g - b] * line
+        inverse.append(state[b] / jnp.sqrt(pivots))
+    inverse = jnp.concatenate(inverse, axis=0)[:, rank:]
 
     factor_ref[...] = exact(mixed, inverse, NT)
     slim = exact(projected, inverse / count, TT)
@@ -264,20 +304,24 @@
         in_specs=[anywhere] * 3,
         out_specs=[inside] * 2,
         scratch_shapes=[
-            pltpu.VMEM((nz, planes, 2 * share, depth), jnp.float32),
+            pltpu.VMEM((4, nz // 2, planes, share, depth), jnp.float32),
             pltpu.VMEM((rank, depth), jnp.float32),
             pltpu.VMEM((2 * width, depth), jnp.bfloat16),
             pltpu.VMEM((share, rank), jnp.float32),
-            pltpu.VMEM((nz, 2 * share, width), jnp.float32),
-            pltpu.VMEM((2 * nz, share, width), jnp.float32),
+            pltpu.VMEM((2, nz // 2, share, width), jnp.float32),
+            pltpu.VMEM((2, nz // 2, share, width), jnp.float32),
+            pltpu.VMEM((2, nz // 2, share, width), jnp.float32),
+            pltpu.VMEM((nz, share, width), jnp.float32),
             pltpu.VMEM((parts, piece, width), jnp.float32),
             pltpu.VMEM((parts, piece, width), jnp.float32),
             pltpu.VMEM((2, 2, longest, piece // 2, width), jnp.float32),
             pltpu.VMEM((parts, piece, width), jnp.float32),
+            dma((4, nz // 2)),
+            dma((2,)),
+            dma((2,)),
+            dma((2,)),
             dma((nz,)),
-            dma((2,)),
-            dma((2 * nz,)),
-            dma((2 * nz,)),
+            dma((nz,)),
             dma((parts,)),
             dma((parts,)),
             dma((2, 2, longest)),
@@ -287,7 +331,7 @@
         ],
         compiler_params=pltpu.CompilerParams(collective_id=0, has_side_effects=True),
         name="exchange",
-    )(field, second_factor.T, first_factor)
+    )(field.reshape(planes, nz, 2, share, depth), second_factor.T, first_factor)
     return pl.pallas_call(
         functools.partial(finish_kernel, float(total_rows)),
         out_shape=(

time: 48.3 us -> 45.1 us (0.934)
  Pallas kernels: 47.5 us -> 44.2 us
    pallas_call x1, Pallas kernels: 7.74 us -> 4.68 us  [on_device(): pl.pallas_call(functools.partial(finish_kernel, float(total_rows)), out_s...]
where the time goes in v3:
time: 45.1 us; the launch traced here: 44.9 us
  Pallas kernels  44.2 us (98%)
  between operations  0.64 us (1%)
    pallas_call x1, Pallas kernels, on_device(): pl.pallas_call(functools.partial(exchange_kernel, nx, ny, nz), out_shape=...  39.6 us
    pallas_call x1, Pallas kernels, on_device(): pl.pallas_call(functools.partial(finish_kernel, float(total_rows)), out_s...  4.68 us

profile of v3, /device:TPU:1, one launch (start us, length us, event | category | flops | bytes accessed | tf_op | source)
XLA Modules:
  0.0 44.9 jit_solution(11067965883264425482)
XLA Ops:
  0.6 39.6 %exchange.1 = (f32[128,128]{1,0:T(8,128)}, f32[16,128]{1,0:T(8,128)}) custom-call(f32[4,8,2,16,512]{4,3,2,1,0:T(8,128)} %bitcast.2, f32[32,512]{1,0:T(8,128)} %bitcast.3, f32[16,32]{1,0:T(8,128)} %first_ref.1), custom_call_target="tpu_custom_call" | custom-call | tf_op jit(solution)/shard_map/exchange/pallas_call | solution.py:298
  40.2 4.7 %finish.1 = (f32[16,32]{1,0:T(8,128)}, f32[32,32,32]{2,1,0:T(8,128)}) custom-call(f32[128,128]{1,0:T(8,128)} %get-tuple-element.4.total_ref, f32[16,128]{1,0:T(8,128)} %get-tuple-element.5.rows_ref, f32[4,32]{1,0:T(4,128)} %third_ref.1), custom_call_target="tpu_custom_call" | custom-call | tf_op jit(solution)/shard_map/finish/pallas_call | solution.py:335

commit v4 on v3

v4 whole, which is shorter than its diff:
```python
import functools

import jax
import jax.numpy as jnp
from jax import lax
from jax.experimental import pallas as pl
from jax.experimental.pallas import tpu as pltpu
from jax.sharding import PartitionSpec as P

HIGHEST = lax.Precision.HIGHEST
MESH = pl.DeviceIdType.MESH
NN = (((1,), (0,)), ((), ()))
NT = (((1,), (1,)), ((), ()))
TN = (((0,), (0,)), ((), ()))
TT = (((0,), (1,)), ((), ()))


def exact(a, b, dims):
    return lax.dot_general(a, b, dims, precision=HIGHEST, preferred_element_type=jnp.float32)


def split(a):
    high = a.astype(jnp.bfloat16)
    return high, (a - high.astype(jnp.float32)).astype(jnp.bfloat16)


def exchange_kernel(
    nx, ny, nz,
    field_ref, second_ref, first_ref, third_ref, total_ref, rows_ref, repeated_ref, kron_ref,
    planes, second, weights, first, partial, paired, outgoing, arrived, local, scattered, stage, third,
    load_sem, small_sem, send_sem, pair_sem, rows_sem, share_sem, stage_sem, final_sem,
):
    gx, gy = lax.axis_index("gx"), lax.axis_index("gy")
    x, y = gx // ny, gx % ny
    z, core = gy // 2, gy % 2
    other = 1 - core
    share = rows_ref.shape[0]
    width = rows_ref.shape[1]
    rank = second_ref.shape[0]
    copies = width // rank
    parts = 2 * nx
    piece = width // parts
    half = piece // 2

    barrier = pltpu.get_barrier_semaphore()
    far_y, far_z, far_x = (sorted(range(n), key=lambda o: -min(o, n - o)) for n in (ny, nz, nx))
    sibling = (gx, z * 2 + other)
    lines = [(x * ny + lax.rem(y + o, ny), gy) for o in far_y if o]
    column = [(gx, lax.rem(z + o, nz) * 2 + core) for o in far_z if o]
    plates = [(lax.rem(x + o, nx) * ny + y, z * 2 + c) for o in far_x if o for c in range(2)]
    peers = lines + column + plates + [sibling]
    for peer in peers:
        pl.semaphore_signal(barrier, inc=1, device_id=peer, device_id_type=MESH)

    group = nz // 2
    owners = [lax.rem(z + o, nz) for o in far_z]
    small = pltpu.make_async_copy(second_ref, second, small_sem.at[0])
    small.start()
    for turn in range(4):
        whose = other if turn < 2 else core
        for j in range(group):
            pltpu.make_async_copy(
                field_ref.at[:, owners[turn % 2 * group + j], whose], planes.at[turn, j], load_sem.at[turn]
            ).start()
    small_first = pltpu.make_async_copy(first_ref, first, small_sem.at[1])
    small_first.start()
    small_third = pltpu.make_async_copy(third_ref, third, small_sem.at[2])
    small_third.start()

    small.wait()
    high, low = split(second[...])
    weights[...] = jnp.concatenate([high] * copies + [low] * copies, axis=0)
    lane = lax.broadcasted_iota(jnp.int32, (group, share, width), 2) // rank

    sends = []
    for turn in range(4):
        pltpu.make_async_copy(planes.at[turn], planes.at[turn], load_sem.at[turn]).wait()
        count = group * copies * share
        block = planes[turn].reshape(count, planes.shape[-1])
        both = jnp.concatenate(split(block), axis=0)
        product = lax.dot_general(both, weights[...], NT, preferred_element_type=jnp.float32)
        acc = product[:count, :width] + (product[:count, width:] + product[count:, :width])
        acc = acc.reshape(group, copies, share, width)
        out = acc[:, 0]
        for k in range(1, copies):
            out = jnp.where(lane == k, acc[:, k], out)
        if turn < 2:
            partial[turn] = out
        if turn == 1:
            pl.semaphore_wait(barrier, len(peers))
            for side in range(2):
                copy = pltpu.make_async_remote_copy(
                    src_ref=partial.at[side],
                    dst_ref=paired.at[side],
                    send_sem=send_sem.at[0],
                    recv_sem=pair_sem.at[side],
                    device_id=sibling,
                    device_id_type=MESH,
                )
                copy.start()
                sends.append(copy)
        if turn >= 2:
            side = turn - 2
            sends[side].wait_recv()
            outgoing[side] = out + paired[side]
            for j in range(group):
                offset = far_z[side * group + j]
                if offset == 0:
                    continue
                pltpu.make_async_remote_copy(
                    src_ref=outgoing.at[side, j],
                    dst_ref=arrived.at[offset],
                    send_sem=send_sem.at[1],
                    recv_sem=rows_sem,
                    device_id=(gx, owners[side * group + j] * 2 + core),
                    device_id_type=MESH,
                ).start()

    small_third.wait()
    repeated = jnp.concatenate(
        [jnp.broadcast_to(third[k : k + 1, :], (rank, rank)) for k in range(copies)], axis=0
    )
    repeated_ref[...] = repeated
    row = lax.broadcasted_iota(jnp.int32, (width, width), 0)
    across = lax.broadcasted_iota(jnp.int32, (width, width), 1)
    kron_ref[...] = jnp.where(row % rank == across % rank, exact(repeated, repeated, NT), 0.0)

    others = pl.ds(1, nz - 1)
    pltpu.make_async_copy(arrived.at[others], arrived.at[others], rows_sem).wait()
    rows = outgoing[1, group - 1]
    for slot in range(1, nz):
        rows = rows + arrived[slot]
    rows_ref[...] = rows

    small_first.wait()
    square = exact(rows, rows, TN)
    probe = exact(first[...], rows, TN)
    second_rows, third_rows, last_rows = (square[k * rank : (k + 1) * rank] for k in range(1, 4))
    corner = lax.broadcasted_iota(jnp.int32, (rank, width), 1) < rank
    packed = jnp.where(corner, pltpu.roll(last_rows, rank, 1), second_rows)
    for at, rows_at in enumerate((square[:rank], packed, third_rows, probe)):
        for j in range(rank // piece):
            local[at * (rank // piece) + j] = rows_at[j * piece : (j + 1) * piece]

    mine = x * 2 + core
    for o in far_x:
        for flip in range(2):
            if o == 0 and flip == 0:
                continue
            to_x, to_core = lax.rem(x + o, nx), lax.rem(core + flip, 2)
            pltpu.make_async_remote_copy(
                src_ref=local.at[to_x * 2 + to_core],
                dst_ref=scattered.at[o * 2 + flip],
                send_sem=send_sem.at[2],
                recv_sem=share_sem,
                device_id=(to_x * ny + y, z * 2 + to_core),
                device_id_type=MESH,
            ).start()
    others = pl.ds(1, parts - 1)
    pltpu.make_async_copy(scattered.at[others], scattered.at[others], share_sem).wait()
    summed = local[mine]
    for slot in range(1, parts):
        summed = summed + scattered[slot]

    halves = [summed[:half], summed[half:]]
    for turn in range(2):
        for h in range(2):
            along_y = (turn + h) % 2 == 0
            me, order = (y, far_y) if along_y else (z, far_z)
            count = len(order)
            stage[turn, h, me] = halves[h]
            for o in order:
                if o == 0:
                    continue
                to = lax.rem(me + o, count)
                pltpu.make_async_remote_copy(
                    src_ref=stage.at[turn, h, me],
                    dst_ref=stage.at[turn, h, me],
                    send_sem=send_sem.at[3 + 2 * turn + h],
                    recv_sem=stage_sem.at[turn, h],
                    device_id=(x * ny + to, gy) if along_y else (gx, to * 2 + core),
                    device_id_type=MESH,
                ).start()
        for h in range(2):
            count = ny if (turn + h) % 2 == 0 else nz
            others = stage.at[turn, h, pl.ds(0, count - 1)]
            pltpu.make_async_copy(others, others, stage_sem.at[turn, h]).wait()
            value = stage[turn, h, 0]
            for j in range(1, count):
                value = value + stage[turn, h, j]
            halves[h] = value

    total_ref[mine, :half] = halves[0]
    total_ref[mine, half:] = halves[1]
    for o in far_x:
        for flip in range(2):
            if o == 0 and flip == 0:
                continue
            pltpu.make_async_remote_copy(
                src_ref=total_ref.at[mine],
                dst_ref=total_ref.at[mine],
                send_sem=send_sem.at[7],
                recv_sem=final_sem,
                device_id=(lax.rem(x + o, nx) * ny + y, z * 2 + lax.rem(core + flip, 2)),
                device_id_type=MESH,
            ).start()
    others = total_ref.at[pl.ds(0, parts - 1)]
    pltpu.make_async_copy(others, others, final_sem).wait()

    sent = [partial, arrived.at[pl.ds(1, nz - 1)], scattered.at[pl.ds(1, parts - 1)]]
    sent += [stage.at[0, 0, pl.ds(0, ny - 1)], stage.at[0, 0, pl.ds(0, nz - 1)]]
    sent += [stage.at[0, 0, pl.ds(0, nz - 1)], stage.at[0, 0, pl.ds(0, ny - 1)], others]
    for at, what in enumerate(sent):
        pltpu.make_async_copy(what, what, send_sem.at[at]).wait()


def finish_kernel(
    count, total_ref, rows_ref, repeated_ref, kron_ref, factor_ref, core_ref,
    factor, core, out_sem,
):
    width, rank = repeated_ref.shape
    planes = width // rank
    kron = kron_ref[...]
    repeated = repeated_ref[...]
    total = total_ref[...].reshape(width, width)
    probe = total[3 * rank :]
    middle = total[rank : 2 * rank]
    zero = jnp.zeros((rank, width), jnp.float32)
    lane = lax.broadcasted_iota(jnp.int32, (rank, width), 1) // rank
    last = jnp.where(lane == 3, pltpu.roll(middle, 3 * rank, 1), zero)
    blocks = [
        total[:rank],
        jnp.where(lane >= 1, middle, zero),
        jnp.where(lane >= 2, total[2 * rank : 3 * rank], zero),
        last,
    ]
    upper = jnp.concatenate(blocks, axis=0)
    strict = jnp.concatenate([jnp.where(lane > k, blocks[k], zero) for k in range(planes)], axis=0)
    weights = exact(probe, kron, NN)
    projected = exact(weights, upper, NN) + exact(weights, strict, NT)
    gram = exact(projected, weights, NT) / count
    mixed = exact(rows_ref[...], weights, NT)

    at = lax.broadcasted_iota(jnp.int32, (rank, rank), 0)
    across = lax.broadcasted_iota(jnp.int32, (rank, rank), 1)
    joined = jnp.concatenate([gram, jnp.where(at == across, 1.0, 0.0)], axis=1)
    size = 8
    groups = rank // size
    shape = (size, 2 * rank)
    state = [joined[g * size : (g + 1) * size] for g in range(groups)]
    below = lax.broadcasted_iota(jnp.int32, shape, 0)
    inverse = []
    for b in range(groups):
        columns = [
            [jnp.broadcast_to(state[g][:, b * size + j : b * size + j + 1], shape) for g in range(b, groups)]
            for j in range(size)
        ]
        pivots = jnp.ones(shape, jnp.float32)
        for j in range(size):
            pivot = jnp.broadcast_to(columns[j][0][j : j + 1], shape)
            pivots = jnp.where(below == j, pivot, pivots)
            scale = 1.0 / pivot
            ratio = [part * scale for part in columns[j]]
            ratio[0] = jnp.where(below > j, ratio[0], 0.0)
            for later in range(j + 1, size):
                top = jnp.broadcast_to(columns[later][0][j : j + 1], shape)
                columns[later] = [part - r * top for part, r in zip(columns[later], ratio)]
            line = jnp.broadcast_to(state[b][j : j + 1], shape)
            for g in range(b, groups):
                state[g] = state[g] - ratio[g - b] * line
        inverse.append(state[b] / jnp.sqrt(pivots))
    inverse = jnp.concatenate(inverse, axis=0)[:, rank:]

    slim = exact(projected, inverse / count, TT)
    factor[...] = exact(mixed, inverse, NT)
    writes = [pltpu.make_async_copy(factor, factor_ref, out_sem.at[0])]
    writes[0].start()
    for c in range(rank):
        terms = slim[:, c : c + 1] * repeated
        core[c] = (terms[:rank] + terms[rank : 2 * rank]) + (terms[2 * rank : 3 * rank] + terms[3 * rank :])
        if c % size == size - 1:
            done = pl.ds(c + 1 - size, size)
            writes.append(pltpu.make_async_copy(core.at[done], core_ref.at[done], out_sem.at[1 + c // size]))
            writes[-1].start()
    for write in writes:
        write.wait()


def on_device(nx, ny, nz, total_rows, field, second_factor, third_factor, first_factor):
    planes, height, depth = field.shape
    rank = second_factor.shape[1]
    share = first_factor.shape[0]
    width = planes * rank
    parts = 2 * nx
    piece = width // parts
    longest = max(ny, nz)
    anywhere = pl.BlockSpec(memory_space=pl.ANY)
    inside = pl.BlockSpec(memory_space=pltpu.VMEM)
    dma = pltpu.SemaphoreType.DMA
    buffers = pl.pallas_call(
        functools.partial(exchange_kernel, nx, ny, nz),
        out_shape=(
            pltpu.VMEM((parts, piece, width), jnp.float32),
            pltpu.VMEM((share, width), jnp.float32),
            pltpu.VMEM((width, rank), jnp.float32),
            pltpu.VMEM((width, width), jnp.float32),
        ),
        in_specs=[anywhere] * 4,
        out_specs=[inside] * 4,
        scratch_shapes=[
            pltpu.VMEM((4, nz // 2, planes, share, depth), jnp.float32),
            pltpu.VMEM((rank, depth), jnp.float32),
            pltpu.VMEM((2 * width, depth), jnp.bfloat16),
            pltpu.VMEM((share, rank), jnp.float32),
            pltpu.VMEM((2, nz // 2, share, width), jnp.float32),
            pltpu.VMEM((2, nz // 2, share, width), jnp.float32),
            pltpu.VMEM((2, nz // 2, share, width), jnp.float32),
            pltpu.VMEM((nz, share, width), jnp.float32),
            pltpu.VMEM((parts, piece, width), jnp.float32),
            pltpu.VMEM((parts, piece, width), jnp.float32),
            pltpu.VMEM((2, 2, longest, piece // 2, width), jnp.float32),
            pltpu.VMEM((planes, rank), jnp.float32),
            dma((4,)),
            dma((3,)),
            dma((8,)),
            dma((2,)),
            dma,
            dma,
            dma((2, 2)),
            dma,
        ],
        compiler_params=pltpu.CompilerParams(collective_id=0, has_side_effects=True),
        name="exchange",
    )(field.reshape(planes, nz, 2, share, depth), second_factor.T, first_factor, third_factor)
    buffers = [pltpu.with_memory_space_constraint(each, pltpu.VMEM) for each in buffers]
    return pl.pallas_call(
        functools.partial(finish_kernel, float(total_rows)),
        out_shape=(
            jax.ShapeDtypeStruct((share, rank), jnp.float32),
            jax.ShapeDtypeStruct((rank, rank, rank), jnp.float32),
        ),
        in_specs=[inside] * 4,
        out_specs=[anywhere] * 2,
        scratch_shapes=[
            pltpu.VMEM((share, rank), jnp.float32),
            pltpu.VMEM((rank, rank, rank), jnp.float32),
            dma((5,)),
        ],
        name="finish",
    )(*buffers)


def build(mesh, nx, ny, nz, total_rows):
    return jax.shard_map(
        functools.partial(on_device, nx, ny, nz, total_rows),
        mesh=mesh,
        in_specs=(P(None, "gx", "gy"), P("gy", None), P(), P(("gx", "gy"), None)),
        out_specs=(P(("gx", "gy"), None), P()),
        check_vma=False,
    )


def solution(mesh):
    ny = 8
    return build(mesh, mesh.shape["gx"] // ny, ny, mesh.shape["gy"] // 2, 8192)
```

time: 45.1 us -> 41.8 us (0.927)
  Pallas kernels: 44.2 us -> 41 us
    pallas_call x1, Pallas kernels: 39.6 us -> 37.6 us  [on_device(): pl.pallas_call(functools.partial(exchange_kernel, nx, ny, nz), out_shape=...]
    pallas_call x1, Pallas kernels: 4.68 us -> 3.44 us  [on_device(): pl.pallas_call(functools.partial(finish_kernel, float(total_rows)), out_s...]
where the time goes in v4:
time: 41.8 us; the launch traced here: 41.7 us
  Pallas kernels  41 us (98%)
  between operations  0.64 us (2%)
    pallas_call x1, Pallas kernels, on_device(): pl.pallas_call(functools.partial(exchange_kernel, nx, ny, nz), out_shape=...  37.6 us
    pallas_call x1, Pallas kernels, on_device(): pl.pallas_call(functools.partial(finish_kernel, float(total_rows)), out_s...  3.44 us

profile of v4, /device:TPU:1, one launch (start us, length us, event | category | flops | bytes accessed | tf_op | source)
XLA Modules:
  0.0 41.7 jit_solution(16135305502486966804)
XLA Ops:
  0.6 37.6 %exchange.1 = (f32[8,16,128]{2,1,0:T(8,128)S(1)}, f32[16,128]{1,0:T(8,128)S(1)}, f32[128,32]{1,0:T(8,128)S(1)}, f32[128,128]{1,0:T(8,128)S(1)}) custom-call(f32[4,8,2,16,512]{4,3,2,1,0:T(8,128)} %bitcast.2, f32[32,512]{1,0:T(8,128)} %bitcast.3, f32[16,32]{1,0:T(8,128)} %first_ref.1, f32[4,32]{1,0:T(4,128)} %third_ref.1), custom_call_target="tpu_custom_call" | custom-call | tf_op jit(solution)/shard_map/exchange/pallas_call | solution.py:300
  38.2 3.4 %finish.1 = (f32[16,32]{1,0:T(8,128)}, f32[32,32,32]{2,1,0:T(8,128)}) custom-call(f32[8,16,128]{2,1,0:T(8,128)S(1)} %get-tuple-element.6.total_ref, f32[16,128]{1,0:T(8,128)S(1)} %get-tuple-element.7.rows_ref, f32[128,32]{1,0:T(8,128)S(1)} %get-tuple-element.8.repeated_ref, f32[128,128]{1,0:T(8,128)S(1)} %get-tuple-element.9.kron_ref), custom_call_target="tpu_custom_call" | custom-call | tf_op jit(solution)/shard_map/finish/pallas_call | solution.py:336

commit v5 on v4

v5 whole, which is shorter than its diff:
```python
import functools

import jax
import jax.numpy as jnp
from jax import lax
from jax.experimental import pallas as pl
from jax.experimental.pallas import tpu as pltpu
from jax.sharding import PartitionSpec as P

HIGHEST = lax.Precision.HIGHEST
MESH = pl.DeviceIdType.MESH
NN = (((1,), (0,)), ((), ()))
NT = (((1,), (1,)), ((), ()))
TN = (((0,), (0,)), ((), ()))
TT = (((0,), (1,)), ((), ()))


def exact(a, b, dims):
    return lax.dot_general(a, b, dims, precision=HIGHEST, preferred_element_type=jnp.float32)


def split(a):
    high = a.astype(jnp.bfloat16)
    return high, (a - high.astype(jnp.float32)).astype(jnp.bfloat16)


def thirds(a):
    high, rest = split_rest(a)
    middle, rest = split_rest(rest)
    return high, middle, rest.astype(jnp.bfloat16)


def split_rest(a):
    high = a.astype(jnp.bfloat16)
    return high, a - high.astype(jnp.float32)


def exchange_kernel(
    nx, ny, nz,
    field_ref, second_ref, first_ref, third_ref, total_ref, rows_ref, repeated_ref, pairs_ref,
    planes, second, weights, first, partial, arrived, local, scattered, stage, third,
    load_sem, small_sem, send_sem, rows_sem, share_sem, stage_sem, final_sem,
):
    gx, gy = lax.axis_index("gx"), lax.axis_index("gy")
    x, y = gx // ny, gx % ny
    z, core = gy // 2, gy % 2
    share = rows_ref.shape[0]
    width = rows_ref.shape[1]
    rank = second_ref.shape[0]
    copies = width // rank
    parts = 2 * nx
    piece = width // parts
    half = piece // 2

    far_y, far_z, far_x = (sorted(range(n), key=lambda o: -min(o, n - o)) for n in (ny, nz, nx))
    group = 2
    turns = nz // group
    hold = min(1, turns - 1)
    owners = [lax.rem(z + o, nz) for o in far_z]
    small = pltpu.make_async_copy(second_ref, second, small_sem.at[0])
    small.start()
    for at in range(nz):
        turn, j = divmod(at, group)
        pltpu.make_async_copy(field_ref.at[:, owners[at]], planes.at[turn, j], load_sem.at[turn]).start()

    barrier = pltpu.get_barrier_semaphore()
    lines = [(x * ny + lax.rem(y + o, ny), gy) for o in far_y if o]
    column = [(gx, lax.rem(z + o, nz) * 2 + lax.rem(core + c, 2)) for o in far_z for c in range(2) if o or c]
    plates = [(lax.rem(x + o, nx) * ny + y, z * 2 + c) for o in far_x if o for c in range(2)]
    peers = lines + column + plates
    for peer in peers:
        pl.semaphore_signal(barrier, inc=1, device_id=peer, device_id_type=MESH)

    small_first = pltpu.make_async_copy(first_ref, first, small_sem.at[1])
    small_first.start()
    small_third = pltpu.make_async_copy(third_ref, third, small_sem.at[2])
    small_third.start()

    small.wait()
    high, low = split(second[...])
    weights[...] = jnp.concatenate([high] * copies + [low] * copies, axis=0)
    lane = lax.broadcasted_iota(jnp.int32, (group, 2 * share, width), 2) // rank

    for turn in range(turns):
        pltpu.make_async_copy(planes.at[turn], planes.at[turn], load_sem.at[turn]).wait()
        count = group * copies * 2 * share
        block = planes[turn].reshape(count, planes.shape[-1])
        high, low = split(block)
        near = lax.dot_general(high, weights[...], NT, preferred_element_type=jnp.float32)
        fine = lax.dot_general(low, weights[:width], NT, preferred_element_type=jnp.float32)
        acc = near[:, :width] + (near[:, width:] + fine)
        acc = acc.reshape(group, copies, 2 * share, width)
        out = acc[:, 0]
        for k in range(1, copies):
            out = jnp.where(lane == k, acc[:, k], out)
        partial[turn] = out.reshape(group, 2, share, width)
        if turn < hold:
            continue
        if turn == hold:
            pl.semaphore_wait(barrier, len(peers))
        for at in range(group * turn if turn > hold else 0, group * (turn + 1)):
            for flip in range(2):
                if far_z[at] == 0 and flip == 0:
                    continue
                target = lax.rem(core + flip, 2)
                pltpu.make_async_remote_copy(
                    src_ref=partial.at[at // group, at % group, target],
                    dst_ref=arrived.at[far_z[at] * 2 + flip],
                    send_sem=send_sem.at[0],
                    recv_sem=rows_sem,
                    device_id=(gx, owners[at] * 2 + target),
                    device_id_type=MESH,
                ).start()

    small_third.wait()
    repeated = jnp.concatenate(
        [jnp.broadcast_to(third[k : k + 1, :], (rank, rank)) for k in range(copies)], axis=0
    )
    repeated_ref[...] = repeated
    products = exact(repeated, repeated, NT)
    block = lax.broadcasted_iota(jnp.int32, (1, width), 1) // rank
    for d in range(copies):
        line = products[0:1]
        for k in range(1, copies):
            line = jnp.where((block + copies - d) % copies == k, products[k * rank : k * rank + 1], line)
        pairs_ref[d : d + 1] = line

    others = pl.ds(1, 2 * nz - 1)
    pltpu.make_async_copy(arrived.at[others], arrived.at[others], rows_sem).wait()
    rows = partial[turns - 1, group - 1, core]
    for slot in range(1, 2 * nz):
        rows = rows + arrived[slot]
    rows_ref[...] = rows

    small_first.wait()
    parts_of = thirds(rows)
    high, middle, low = parts_of
    left = [jnp.concatenate([a, b], axis=1) for a, b in zip(parts_of, thirds(first[...]))]
    left = jnp.concatenate([left[at] for at in (0, 0, 1, 1, 0, 2)], axis=0)
    right = jnp.concatenate([high, middle, high, middle, low, high], axis=0)
    both = lax.dot_general(left, right, TN, preferred_element_type=jnp.float32)
    square, probe = both[:width], both[width:]
    second_rows, third_rows, last_rows = (square[k * rank : (k + 1) * rank] for k in range(1, 4))
    corner = lax.broadcasted_iota(jnp.int32, (rank, width), 1) < rank
    packed = jnp.where(corner, pltpu.roll(last_rows, rank, 1), second_rows)
    for at, rows_at in enumerate((square[:rank], packed, third_rows, probe)):
        for j in range(rank // piece):
            local[at * (rank // piece) + j] = rows_at[j * piece : (j + 1) * piece]

    mine = x * 2 + core
    for o in far_x:
        for flip in range(2):
            if o == 0 and flip == 0:
                continue
            to_x, to_core = lax.rem(x + o, nx), lax.rem(core + flip, 2)
            pltpu.make_async_remote_copy(
                src_ref=local.at[to_x * 2 + to_core],
                dst_ref=scattered.at[o * 2 + flip],
                send_sem=send_sem.at[1],
                recv_sem=share_sem,
                device_id=(to_x * ny + y, z * 2 + to_core),
                device_id_type=MESH,
            ).start()
    others = pl.ds(1, parts - 1)
    pltpu.make_async_copy(scattered.at[others], scattered.at[others], share_sem).wait()
    summed = local[mine]
    for slot in range(1, parts):
        summed = summed + scattered[slot]

    def send_half(turn, h, value):
        along_y = (turn + h) % 2 == 0
        me, order = (y, far_y) if along_y else (z, far_z)
        stage[turn, h, me] = value
        for o in order:
            if o == 0:
                continue
            to = lax.rem(me + o, len(order))
            pltpu.make_async_remote_copy(
                src_ref=stage.at[turn, h, me],
                dst_ref=stage.at[turn, h, me],
                send_sem=send_sem.at[2 + 2 * turn + h],
                recv_sem=stage_sem.at[turn, h],
                device_id=(x * ny + to, gy) if along_y else (gx, to * 2 + core),
                device_id_type=MESH,
            ).start()

    def sum_half(turn, h):
        count = ny if (turn + h) % 2 == 0 else nz
        arriving = stage.at[turn, h, pl.ds(0, count - 1)]
        pltpu.make_async_copy(arriving, arriving, stage_sem.at[turn, h]).wait()
        value = stage[turn, h, 0]
        for j in range(1, count):
            value = value + stage[turn, h, j]
        return value

    for h in range(2):
        send_half(0, h, summed[h * half : (h + 1) * half])
    for h in range(2):
        send_half(1, h, sum_half(0, h))
    for h in range(2):
        span = pl.ds(h * half, half)
        total_ref[mine, span] = sum_half(1, h)
        for o in far_x:
            for flip in range(2):
                if o == 0 and flip == 0:
                    continue
                pltpu.make_async_remote_copy(
                    src_ref=total_ref.at[mine, span],
                    dst_ref=total_ref.at[mine, span],
                    send_sem=send_sem.at[6],
                    recv_sem=final_sem,
                    device_id=(lax.rem(x + o, nx) * ny + y, z * 2 + lax.rem(core + flip, 2)),
                    device_id_type=MESH,
                ).start()
    others = total_ref.at[pl.ds(0, parts - 1)]
    pltpu.make_async_copy(others, others, final_sem).wait()

    sent = [arrived.at[pl.ds(1, 2 * nz - 1)], scattered.at[pl.ds(1, parts - 1)]]
    sent += [stage.at[0, 0, pl.ds(0, ny - 1)], stage.at[0, 0, pl.ds(0, nz - 1)]]
    sent += [stage.at[0, 0, pl.ds(0, nz - 1)], stage.at[0, 0, pl.ds(0, ny - 1)], others]
    for at, what in enumerate(sent):
        pltpu.make_async_copy(what, what, send_sem.at[at]).wait()


def finish_kernel(
    count, total_ref, rows_ref, repeated_ref, pairs_ref, factor_ref, core_ref,
    factor, core, out_sem,
):
    width, rank = repeated_ref.shape
    planes = width // rank
    repeated = repeated_ref[...]
    total = total_ref[...].reshape(width, width)
    probe = total[3 * rank :]
    middle = total[rank : 2 * rank]
    zero = jnp.zeros((rank, width), jnp.float32)
    lane = lax.broadcasted_iota(jnp.int32, (rank, width), 1) // rank
    last = jnp.where(lane == 3, pltpu.roll(middle, 3 * rank, 1), zero)
    blocks = [
        total[:rank],
        jnp.where(lane >= 1, middle, zero),
        jnp.where(lane >= 2, total[2 * rank : 3 * rank], zero),
        last,
    ]
    upper = jnp.concatenate(blocks, axis=0)
    strict = jnp.concatenate([jnp.where(lane > k, blocks[k], zero) for k in range(planes)], axis=0)
    weights = probe * pairs_ref[0:1]
    for d in range(1, planes):
        weights = weights + pltpu.roll(probe, d * rank, 1) * pairs_ref[d : d + 1]
    projected = exact(weights, upper, NN) + exact(weights, strict, NT)
    gram = exact(projected, weights, NT) / count
    mixed = exact(rows_ref[...], weights, NT)

    at = lax.broadcasted_iota(jnp.int32, (rank, rank), 0)
    across = lax.broadcasted_iota(jnp.int32, (rank, rank), 1)
    joined = jnp.concatenate([gram, jnp.where(at == across, 1.0, 0.0)], axis=1)
    size = 8
    groups = rank // size
    shape = (size, 2 * rank)
    state = [joined[g * size : (g + 1) * size] for g in range(groups)]
    below = lax.broadcasted_iota(jnp.int32, shape, 0)
    inverse = []
    for b in range(groups):
        columns = [
            [jnp.broadcast_to(state[g][:, b * size + j : b * size + j + 1], shape) for g in range(b, groups)]
            for j in range(size)
        ]
        pivots = jnp.ones(shape, jnp.float32)
        for j in range(size):
            pivot = jnp.broadcast_to(columns[j][0][j : j + 1], shape)
            pivots = jnp.where(below == j, pivot, pivots)
            scale = 1.0 / pivot
            ratio = [part * scale for part in columns[j]]
            ratio[0] = jnp.where(below > j, ratio[0], 0.0)
            for later in range(j + 1, size):
                top = jnp.broadcast_to(columns[later][0][j : j + 1], shape)
                columns[later] = [part - r * top for part, r in zip(columns[later], ratio)]
            line = jnp.broadcast_to(state[b][j : j + 1], shape)
            for g in range(b, groups):
                state[g] = state[g] - ratio[g - b] * line
        inverse.append(state[b] / jnp.sqrt(pivots))
    inverse = jnp.concatenate(inverse, axis=0)[:, rank:]

    slim = exact(inverse / count, projected, NN)
    factor[...] = exact(mixed, inverse, NT)
    writes = [pltpu.make_async_copy(factor, factor_ref, out_sem.at[0])]
    writes[0].start()
    third_high, third_low = split(repeated)
    keep = lax.broadcasted_iota(jnp.int32, (rank, width), 1) % rank == lax.broadcasted_iota(
        jnp.int32, (rank, width), 0
    )
    for g in range(groups):
        spread = jnp.concatenate(
            [
                jnp.where(keep, jnp.broadcast_to(slim[c : c + 1], (rank, width)), 0.0)
                for c in range(g * size, (g + 1) * size)
            ],
            axis=0,
        )
        high, low = split(spread)
        near = lax.dot_general(high, third_high, NN, preferred_element_type=jnp.float32)
        fine = lax.dot_general(high, third_low, NN, preferred_element_type=jnp.float32)
        fine = fine + lax.dot_general(low, third_high, NN, preferred_element_type=jnp.float32)
        done = pl.ds(g * size, size)
        core[done] = (near + fine).reshape(size, rank, rank)
        writes.append(pltpu.make_async_copy(core.at[done], core_ref.at[done], out_sem.at[1 + g]))
        writes[-1].start()
    for write in writes:
        write.wait()


def on_device(nx, ny, nz, total_rows, field, second_factor, third_factor, first_factor):
    planes, height, depth = field.shape
    rank = second_factor.shape[1]
    share = first_factor.shape[0]
    width = planes * rank
    parts = 2 * nx
    piece = width // parts
    longest = max(ny, nz)
    anywhere = pl.BlockSpec(memory_space=pl.ANY)
    inside = pl.BlockSpec(memory_space=pltpu.VMEM)
    dma = pltpu.SemaphoreType.DMA
    buffers = pl.pallas_call(
        functools.partial(exchange_kernel, nx, ny, nz),
        out_shape=(
            pltpu.VMEM((parts, piece, width), jnp.float32),
            pltpu.VMEM((share, width), jnp.float32),
            pltpu.VMEM((width, rank), jnp.float32),
            pltpu.VMEM((planes, width), jnp.float32),
        ),
        in_specs=[anywhere] * 4,
        out_specs=[inside] * 4,
        scratch_shapes=[
            pltpu.VMEM((nz // 2, 2, planes, 2 * share, depth), jnp.float32),
            pltpu.VMEM((rank, depth), jnp.float32),
            pltpu.VMEM((2 * width, depth), jnp.bfloat16),
            pltpu.VMEM((share, rank), jnp.float32),
            pltpu.VMEM((nz // 2, 2, 2, share, width), jnp.float32),
            pltpu.VMEM((2 * nz, share, width), jnp.float32),
            pltpu.VMEM((parts, piece, width), jnp.float32),
            pltpu.VMEM((parts, piece, width), jnp.float32),
            pltpu.VMEM((2, 2, longest, piece // 2, width), jnp.float32),
            pltpu.VMEM((planes, rank), jnp.float32),
            dma((nz // 2,)),
            dma((3,)),
            dma((7,)),
            dma,
            dma,
            dma((2, 2)),
            dma,
        ],
        compiler_params=pltpu.CompilerParams(collective_id=0, has_side_effects=True),
        name="exchange",
    )(field.reshape(planes, nz, 2 * share, depth), second_factor.T, first_factor, third_factor)
    buffers = [pltpu.with_memory_space_constraint(each, pltpu.VMEM) for each in buffers]
    return pl.pallas_call(
        functools.partial(finish_kernel, float(total_rows)),
        out_shape=(
            jax.ShapeDtypeStruct((share, rank), jnp.float32),
            jax.ShapeDtypeStruct((rank, rank, rank), jnp.float32),
        ),
        in_specs=[inside] * 4,
        out_specs=[anywhere] * 2,
        scratch_shapes=[
            pltpu.VMEM((share, rank), jnp.float32),
            pltpu.VMEM((rank, rank, rank), jnp.float32),
            dma((5,)),
        ],
        name="finish",
    )(*buffers)


def build(mesh, nx, ny, nz, total_rows):
    return jax.shard_map(
        functools.partial(on_device, nx, ny, nz, total_rows),
        mesh=mesh,
        in_specs=(P(None, "gx", "gy"), P("gy", None), P(), P(("gx", "gy"), None)),
        out_specs=(P(("gx", "gy"), None), P()),
        check_vma=False,
    )


def solution(mesh):
    ny = 8
    return build(mesh, mesh.shape["gx"] // ny, ny, mesh.shape["gy"] // 2, 8192)
```

time: 41.8 us -> 41.4 us (level)
    pallas_call x1, Pallas kernels: 3.44 us -> 2.75 us  [on_device(): pl.pallas_call(functools.partial(finish_kernel, float(total_rows)), out_s...]
where the time goes in v5:
time: 41.4 us; the launch traced here: 41.3 us
  Pallas kernels  40.7 us (98%)
  between operations  0.64 us (2%)
    pallas_call x1, Pallas kernels, on_device(): pl.pallas_call(functools.partial(exchange_kernel, nx, ny, nz), out_shape=...  37.9 us
    pallas_call x1, Pallas kernels, on_device(): pl.pallas_call(functools.partial(finish_kernel, float(total_rows)), out_s...  2.75 us

profile of v5, /device:TPU:1, one launch (start us, length us, event | category | flops | bytes accessed | tf_op | source)
XLA Modules:
  0.0 41.3 jit_solution(15835769708706724685)
XLA Ops:
  0.6 37.9 %exchange.1 = (f32[8,16,128]{2,1,0:T(8,128)S(1)}, f32[16,128]{1,0:T(8,128)S(1)}, f32[128,32]{1,0:T(8,128)S(1)}, f32[4,128]{1,0:T(4,128)S(1)}) custom-call(f32[4,8,32,512]{3,2,1,0:T(8,128)} %bitcast.2, f32[32,512]{1,0:T(8,128)} %bitcast.3, f32[16,32]{1,0:T(8,128)} %first_ref.1, f32[4,32]{1,0:T(4,128)} %third_ref.1), custom_call_target="tpu_custom_call" | custom-call | tf_op jit(solution)/shard_map/exchange/pallas_call | solution.py:322
  38.5 2.8 %finish.1 = (f32[16,32]{1,0:T(8,128)}, f32[32,32,32]{2,1,0:T(8,128)}) custom-call(f32[8,16,128]{2,1,0:T(8,128)S(1)} %get-tuple-element.6.total_ref, f32[16,128]{1,0:T(8,128)S(1)} %get-tuple-element.7.rows_ref, f32[128,32]{1,0:T(8,128)S(1)} %get-tuple-element.8.repeated_ref, f32[4,128]{1,0:T(4,128)S(1)} %get-tuple-element.9.pairs_ref), custom_call_target="tpu_custom_call" | custom-call | tf_op jit(solution)/shard_map/finish/pallas_call | solution.py:355

commit v6 on v5

--- a/solution.py
+++ b/solution.py
@@ -259,25 +259,29 @@
     state = [joined[g * size : (g + 1) * size] for g in range(groups)]
     below = lax.broadcasted_iota(jnp.int32, shape, 0)
     inverse = []
-    for b in range(groups):
+    wide = 16
+    for b in range(rank // wide):
+        head = b * wide // size
         columns = [
-            [jnp.broadcast_to(state[g][:, b * size + j : b * size + j + 1], shape) for g in range(b, groups)]
-            for j in range(size)
+            [jnp.broadcast_to(state[g][:, b * wide + j : b * wide + j + 1], shape) for g in range(groups)]
+            for j in range(wide)
         ]
-        pivots = jnp.ones(shape, jnp.float32)
-        for j in range(size):
-            pivot = jnp.broadcast_to(columns[j][0][j : j + 1], shape)
-            pivots = jnp.where(below == j, pivot, pivots)
+        for j in range(wide):
+            at, spot = head + j // size, j % size
+            pivot = jnp.broadcast_to(columns[j][at][spot : spot + 1], shape)
+            pivots = jnp.where(below == spot, pivot, pivots if spot else jnp.ones(shape, jnp.float32))
             scale = 1.0 / pivot
-            ratio = [part * scale for part in columns[j]]
-            ratio[0] = jnp.where(below > j, ratio[0], 0.0)
-            for later in range(j + 1, size):
-                top = jnp.broadcast_to(columns[later][0][j : j + 1], shape)
-                columns[later] = [part - r * top for part, r in zip(columns[later], ratio)]
-            line = jnp.broadcast_to(state[b][j : j + 1], shape)
-            for g in range(b, groups):
-                state[g] = state[g] - ratio[g - b] * line
-        inverse.append(state[b] / jnp.sqrt(pivots))
+            ratio = {g: columns[j][g] * scale for g in range(at, groups)}
+            ratio[at] = jnp.where(below > spot, ratio[at], 0.0)
+            for later in range(j + 1, wide):
+                top = jnp.broadcast_to(columns[later][at][spot : spot + 1], shape)
+                for g in range(at, groups):
+                    columns[later][g] = columns[later][g] - ratio[g] * top
+            line = jnp.broadcast_to(state[at][spot : spot + 1], shape)
+            for g in range(at, groups):
+                state[g] = state[g] - ratio[g] * line
+            if spot == size - 1:
+                inverse.append(state[at] / jnp.sqrt(pivots))
     inverse = jnp.concatenate(inverse, axis=0)[:, rank:]
 
     slim = exact(inverse / count, projected, NN)

time: 41.4 us -> 41.3 us (level)
  no operation moved by 1% of the time
where the time goes in v6:
time: 41.3 us; the launch traced here: 41.1 us
  Pallas kernels  40.5 us (98%)
  between operations  0.64 us (2%)
    pallas_call x1, Pallas kernels, on_device(): pl.pallas_call(functools.partial(exchange_kernel, nx, ny, nz), out_shape=...  37.9 us
    pallas_call x1, Pallas kernels, on_device(): pl.pallas_call(functools.partial(finish_kernel, float(total_rows)), out_s...  2.61 us

profile of v6, /device:TPU:1, one launch (start us, length us, event | category | flops | bytes accessed | tf_op | source)
XLA Modules:
  0.0 41.1 jit_solution(310553757062127165)
XLA Ops:
  0.6 37.9 %exchange.1 = (f32[8,16,128]{2,1,0:T(8,128)S(1)}, f32[16,128]{1,0:T(8,128)S(1)}, f32[128,32]{1,0:T(8,128)S(1)}, f32[4,128]{1,0:T(4,128)S(1)}) custom-call(f32[4,8,32,512]{3,2,1,0:T(8,128)} %bitcast.2, f32[32,512]{1,0:T(8,128)} %bitcast.3, f32[16,32]{1,0:T(8,128)} %first_ref.1, f32[4,32]{1,0:T(4,128)} %third_ref.1), custom_call_target="tpu_custom_call" | custom-call | tf_op jit(solution)/shard_map/exchange/pallas_call | solution.py:326
  38.5 2.6 %finish.1 = (f32[16,32]{1,0:T(8,128)}, f32[32,32,32]{2,1,0:T(8,128)}) custom-call(f32[8,16,128]{2,1,0:T(8,128)S(1)} %get-tuple-element.6.total_ref, f32[16,128]{1,0:T(8,128)S(1)} %get-tuple-element.7.rows_ref, f32[128,32]{1,0:T(8,128)S(1)} %get-tuple-element.8.repeated_ref, f32[4,128]{1,0:T(4,128)S(1)} %get-tuple-element.9.pairs_ref), custom_call_target="tpu_custom_call" | custom-call | tf_op jit(solution)/shard_map/finish/pallas_call | solution.py:359

commit v7 on v6

--- a/solution.py
+++ b/solution.py
@@ -198,20 +198,19 @@
     for h in range(2):
         send_half(1, h, sum_half(0, h))
     for h in range(2):
-        span = pl.ds(h * half, half)
-        total_ref[mine, span] = sum_half(1, h)
-        for o in far_x:
-            for flip in range(2):
-                if o == 0 and flip == 0:
-                    continue
-                pltpu.make_async_remote_copy(
-                    src_ref=total_ref.at[mine, span],
-                    dst_ref=total_ref.at[mine, span],
-                    send_sem=send_sem.at[6],
-                    recv_sem=final_sem,
-                    device_id=(lax.rem(x + o, nx) * ny + y, z * 2 + lax.rem(core + flip, 2)),
-                    device_id_type=MESH,
-                ).start()
+        total_ref[mine, pl.ds(h * half, half)] = sum_half(1, h)
+    for o in far_x:
+        for flip in range(2):
+            if o == 0 and flip == 0:
+                continue
+            pltpu.make_async_remote_copy(
+                src_ref=total_ref.at[mine],
+                dst_ref=total_ref.at[mine],
+                send_sem=send_sem.at[6],
+                recv_sem=final_sem,
+                device_id=(lax.rem(x + o, nx) * ny + y, z * 2 + lax.rem(core + flip, 2)),
+                device_id_type=MESH,
+            ).start()
     others = total_ref.at[pl.ds(0, parts - 1)]
     pltpu.make_async_copy(others, others, final_sem).wait()
 
@@ -260,6 +259,26 @@
     below = lax.broadcasted_iota(jnp.int32, shape, 0)
     inverse = []
     wide = 16
+    writes = []
+    third_high, third_low = split(repeated)
+    keep = lax.broadcasted_iota(jnp.int32, (rank, width), 1) % rank == lax.broadcasted_iota(
+        jnp.int32, (rank, width), 0
+    )
+
+    def write_core(g):
+        slim = exact(inverse[g][:, rank:] / count, projected, NN)
+        spread = jnp.concatenate(
+            [jnp.where(keep, jnp.broadcast_to(slim[c : c + 1], (rank, width)), 0.0) for c in range(size)], axis=0
+        )
+        high, low = split(spread)
+        near = lax.dot_general(high, third_high, NN, preferred_element_type=jnp.float32)
+        fine = lax.dot_general(high, third_low, NN, preferred_element_type=jnp.float32)
+        fine = fine + lax.dot_general(low, third_high, NN, preferred_element_type=jnp.float32)
+        done = pl.ds(g * size, size)
+        core[done] = (near + fine).reshape(size, rank, rank)
+        writes.append(pltpu.make_async_copy(core.at[done], core_ref.at[done], out_sem.at[1 + g]))
+        writes[-1].start()
+
     for b in range(rank // wide):
         head = b * wide // size
         columns = [
@@ -282,32 +301,12 @@
                 state[g] = state[g] - ratio[g] * line
             if spot == size - 1:
                 inverse.append(state[at] / jnp.sqrt(pivots))
+                write_core(at)
     inverse = jnp.concatenate(inverse, axis=0)[:, rank:]
 
-    slim = exact(inverse / count, projected, NN)
     factor[...] = exact(mixed, inverse, NT)
-    writes = [pltpu.make_async_copy(factor, factor_ref, out_sem.at[0])]
-    writes[0].start()
-    third_high, third_low = split(repeated)
-    keep = lax.broadcasted_iota(jnp.int32, (rank, width), 1) % rank == lax.broadcasted_iota(
-        jnp.int32, (rank, width), 0
-    )
-    for g in range(groups):
-        spread = jnp.concatenate(
-            [
-                jnp.where(keep, jnp.broadcast_to(slim[c : c + 1], (rank, width)), 0.0)
-                for c in range(g * size, (g + 1) * size)
-            ],
-            axis=0,
-        )
-        high, low = split(spread)
-        near = lax.dot_general(high, third_high, NN, preferred_element_type=jnp.float32)
-        fine = lax.dot_general(high, third_low, NN, preferred_element_type=jnp.float32)
-        fine = fine + lax.dot_general(low, third_high, NN, preferred_element_type=jnp.float32)
-        done = pl.ds(g * size, size)
-        core[done] = (near + fine).reshape(size, rank, rank)
-        writes.append(pltpu.make_async_copy(core.at[done], core_ref.at[done], out_sem.at[1 + g]))
-        writes[-1].start()
+    writes.append(pltpu.make_async_copy(factor, factor_ref, out_sem.at[0]))
+    writes[-1].start()
     for write in writes:
         write.wait()
 

time: 41.3 us -> 41.1 us (level)
  no operation moved by 1% of the time
where the time goes in v7:
time: 41.1 us; the launch traced here: 41 us
  Pallas kernels  40.3 us (98%)
  between operations  0.64 us (2%)
    pallas_call x1, Pallas kernels, on_device(): pl.pallas_call(functools.partial(exchange_kernel, nx, ny, nz), out_shape=...  37.8 us
    pallas_call x1, Pallas kernels, on_device(): pl.pallas_call(functools.partial(finish_kernel, float(total_rows)), out_s...  2.57 us

profile of v7, /device:TPU:1, one launch (start us, length us, event | category | flops | bytes accessed | tf_op | source)
XLA Modules:
  0.0 41.0 jit_solution(17903605197357641522)
XLA Ops:
  0.6 37.8 %exchange.1 = (f32[8,16,128]{2,1,0:T(8,128)S(1)}, f32[16,128]{1,0:T(8,128)S(1)}, f32[128,32]{1,0:T(8,128)S(1)}, f32[4,128]{1,0:T(4,128)S(1)}) custom-call(f32[4,8,32,512]{3,2,1,0:T(8,128)} %bitcast.2, f32[32,512]{1,0:T(8,128)} %bitcast.3, f32[16,32]{1,0:T(8,128)} %first_ref.1, f32[4,32]{1,0:T(4,128)} %third_ref.1), custom_call_target="tpu_custom_call" | custom-call | tf_op jit(solution)/shard_map/exchange/pallas_call | solution.py:325
  38.4 2.6 %finish.1 = (f32[16,32]{1,0:T(8,128)}, f32[32,32,32]{2,1,0:T(8,128)}) custom-call(f32[8,16,128]{2,1,0:T(8,128)S(1)} %get-tuple-element.6.total_ref, f32[16,128]{1,0:T(8,128)S(1)} %get-tuple-element.7.rows_ref, f32[128,32]{1,0:T(8,128)S(1)} %get-tuple-element.8.repeated_ref, f32[4,128]{1,0:T(4,128)S(1)} %get-tuple-element.9.pairs_ref), custom_call_target="tpu_custom_call" | custom-call | tf_op jit(solution)/shard_map/finish/pallas_call | solution.py:358

commit v8 on v6

--- a/solution.py
+++ b/solution.py
@@ -55,7 +55,7 @@
     far_y, far_z, far_x = (sorted(range(n), key=lambda o: -min(o, n - o)) for n in (ny, nz, nx))
     group = 2
     turns = nz // group
-    hold = min(1, turns - 1)
+    hold = 0
     owners = [lax.rem(z + o, nz) for o in far_z]
     small = pltpu.make_async_copy(second_ref, second, small_sem.at[0])
     small.start()

time: 41.3 us -> 41.3 us (level)
  no operation moved by 1% of the time
where the time goes in v8:
time: 41.3 us; the launch traced here: 41.2 us
  Pallas kernels  40.5 us (98%)
  between operations  0.64 us (2%)
    pallas_call x1, Pallas kernels, on_device(): pl.pallas_call(functools.partial(exchange_kernel, nx, ny, nz), out_shape=...  37.9 us
    pallas_call x1, Pallas kernels, on_device(): pl.pallas_call(functools.partial(finish_kernel, float(total_rows)), out_s...  2.6 us

profile of v8, /device:TPU:1, one launch (start us, length us, event | category | flops | bytes accessed | tf_op | source)
XLA Modules:
  0.0 41.2 jit_solution(5299258928365543452)
XLA Ops:
  0.6 37.9 %exchange.1 = (f32[8,16,128]{2,1,0:T(8,128)S(1)}, f32[16,128]{1,0:T(8,128)S(1)}, f32[128,32]{1,0:T(8,128)S(1)}, f32[4,128]{1,0:T(4,128)S(1)}) custom-call(f32[4,8,32,512]{3,2,1,0:T(8,128)} %bitcast.2, f32[32,512]{1,0:T(8,128)} %bitcast.3, f32[16,32]{1,0:T(8,128)} %first_ref.1, f32[4,32]{1,0:T(4,128)} %third_ref.1), custom_call_target="tpu_custom_call" | custom-call | tf_op jit(solution)/shard_map/exchange/pallas_call | solution.py:326
  38.6 2.6 %finish.1 = (f32[16,32]{1,0:T(8,128)}, f32[32,32,32]{2,1,0:T(8,128)}) custom-call(f32[8,16,128]{2,1,0:T(8,128)S(1)} %get-tuple-element.6.total_ref, f32[16,128]{1,0:T(8,128)S(1)} %get-tuple-element.7.rows_ref, f32[128,32]{1,0:T(8,128)S(1)} %get-tuple-element.8.repeated_ref, f32[4,128]{1,0:T(4,128)S(1)} %get-tuple-element.9.pairs_ref), custom_call_target="tpu_custom_call" | custom-call | tf_op jit(solution)/shard_map/finish/pallas_call | solution.py:359
